TPU v7x, 128 devices: a whole 4x4x4 slice. The times are simulated.
128 devices in a mesh: row: 8 (over x, core), col: 16 (over z, y).
Axes of the slice: x: 4, y: 4, z: 4, core: 2. Of those that a mesh axis runs over, the one named last changes fastest.
Arguments:
- hamiltonian: float32 [256, 4, 128, 128], P(('row', 'col')), may hold values from -20 to 20
- block_lists: int32 [256, 4], replicated, may hold values from -1 to 255, as said below
Outputs:
- density: float32 [256, 4, 128, 128], P(('row', 'col'))
Inputs may be any that keep to these rules, and one draw needn't show every extreme that they name: `block_lists`: block column j = (r * 16 + c) * 2 + s sits on grid row r, grid column c, slot s. Entry 0 is j. Entry 1 is the column of the same r and s at grid column c - 1 (cyclically), entry 2 the one at c + 1, each either present or -1, present for both ends of a link or for neither. Entry 3 is never -1: the column of the same c and s on grid row r with one bit flipped, the same bit for all rows of one grid column and slot. Some columns have all four entries, some only entries 0 and 3.
All inputs are finite; a program needn't handle non-finite values.
Results may differ from a plain program's by a relative error of at most 0.0001.
Values sent between devices are 32-bit elements; how exact they have to be, the bound alone decides.
A program may use at most 64 MiB of HBM per device.

v0:
```python
import jax
import jax.numpy as jnp
from jax import lax
from jax.sharding import PartitionSpec as P

ITERS = 6
STEPS = 2


epsilon = 1e-06


def with_halo(block, sides, width):
    for axis, dim in sides:
        count = lax.axis_size(axis)
        forward = [(i, i + 1) for i in range(count - 1)]
        forward.append((count - 1, 0))
        backward = [(target, source) for source, target in forward]
        low = lax.ppermute(
            lax.slice_in_dim(block, block.shape[dim] - width, None, axis=dim), axis, forward
        )
        high = lax.ppermute(lax.slice_in_dim(block, 0, width, axis=dim), axis, backward)
        block = jnp.concatenate([low, block, high], axis=dim)
    return block


def symmetric(matrix):
    return 0.5 * (matrix + jnp.swapaxes(matrix, -1, -2))


def assemble(own_col, diagonals, face_blocks, present):
    column = 0.5 * (own_col + jnp.swapaxes(face_blocks, -1, -2)) * present[:, None, None]
    blocks = symmetric(diagonals) * present[:, None, None]
    side_len = own_col.shape[-1]
    members = own_col.shape[0]
    matrix = jnp.zeros((members, side_len, members, side_len), jnp.float32)
    matrix = matrix.at[0, :, 0, :].set(column[0])
    for position in range(1, members):
        matrix = matrix.at[position, :, 0, :].set(column[position])
        matrix = matrix.at[0, :, position, :].set(column[position].T)
        matrix = matrix.at[position, :, position, :].set(blocks[position])
    return matrix.reshape(members * side_len, members * side_len)


def sign_batch(matrices, first_squares, scaling, present):
    slots_here = matrices.shape[0]
    full_order = matrices.shape[1]
    members = present.shape[1]
    side_len = full_order // members
    identity = jnp.eye(full_order, dtype=jnp.float32)
    iterate = matrices * scaling
    square = first_squares * (scaling * scaling)
    for repeat in range(ITERS):
        if repeat > 0:
            square = jnp.einsum("sab,sbc->sac", iterate, iterate, precision=lax.Precision.HIGHEST)
        iterate = jnp.einsum(
            "sab,sbc->sac", iterate, 1.5 * identity - 0.5 * square, precision=lax.Precision.HIGHEST
        )
    central = 0.5 * (identity[:, :side_len] - iterate[:, :, :side_len])
    return central.reshape(slots_here, members, side_len, side_len) * present[:, :, None, None]


def per_device(hamiltonian, block_lists):
    slots_here = hamiltonian.shape[0]
    cycle_size = lax.axis_size("col")
    my_row = lax.axis_index("row")
    device = my_row * cycle_size + lax.axis_index("col")
    my_lists = lax.dynamic_slice_in_dim(block_lists, device * slots_here, slots_here, 0)
    present = (my_lists >= 0).astype(jnp.float32)
    partner_row = my_lists[:, 3] // slots_here // cycle_size
    slot_ids = jnp.arange(slots_here, dtype=jnp.int32)
    cycle_cols = with_halo(hamiltonian[None], (("col", 0),), 1)
    stored_left_diag = cycle_cols[0][:, 0]
    stored_left_face = cycle_cols[0][:, 2]
    stored_right_diag = cycle_cols[2][:, 0]
    stored_right_face = cycle_cols[2][:, 1]
    partner_pos = 3
    everyone = lax.all_gather(hamiltonian[None], "row", axis=0, tiled=True)
    partner = everyone[partner_row, slot_ids]
    stored_part_diag = partner[:, 0]
    stored_part_face = partner[:, partner_pos]
    left_diag, left_face = (stored_left_diag, stored_left_face)
    right_diag, right_face = (stored_right_diag, stored_right_face)
    part_diag, part_face = (stored_part_diag, stored_part_face)
    current = hamiltonian
    density = hamiltonian
    for scf_round in range(STEPS):
        diagonals = jnp.stack((current[:, 0], left_diag, right_diag, part_diag), 1)
        face_blocks = jnp.stack((current[:, 0], left_face, right_face, part_face), 1)
        matrices = jax.vmap(assemble)(current, diagonals, face_blocks, present)
        first_squares = jnp.einsum(
            "sab,sbc->sac", matrices, matrices, precision=lax.Precision.HIGHEST
        )
        local_top = jnp.max(jnp.sum(first_squares * first_squares, axis=(1, 2)))
        largest = lax.pmax(local_top, ("row", "col"))
        scaling = 1.5 / jnp.sqrt(jnp.sqrt(largest + epsilon))
        density_cols = sign_batch(matrices, first_squares, scaling, present)
        cycle_dens = with_halo(density_cols[None], (("col", 0),), 1)
        left_dens = cycle_dens[0][:, 2]
        left_centre = cycle_dens[0][:, 0]
        right_dens = cycle_dens[2][:, 1]
        right_centre = cycle_dens[2][:, 0]
        sent_partner = jnp.stack((density_cols[:, 3], density_cols[:, 0]), 1)
        everyone_dens = lax.all_gather(sent_partner[None], "row", axis=0, tiled=True)
        partner_pair = everyone_dens[partner_row, slot_ids]
        partner_dens = partner_pair[:, 0]
        partner_centre = partner_pair[:, 1]
        density_face = jnp.stack((density_cols[:, 0], left_dens, right_dens, partner_dens), 1)
        density = (
            0.5 * (density_cols + jnp.swapaxes(density_face, -1, -2)) * present[:, :, None, None]
        )
        if scf_round + 1 < STEPS:
            current = hamiltonian + density
            density_turned = jnp.swapaxes(density, -1, -2)
            left_diag = stored_left_diag + symmetric(left_centre)
            right_diag = stored_right_diag + symmetric(right_centre)
            part_diag = stored_part_diag + symmetric(partner_centre)
            left_face = stored_left_face + density_turned[:, 1]
            right_face = stored_right_face + density_turned[:, 2]
            part_face = stored_part_face + density_turned[:, 3]
    return density


def solution(mesh):
    return jax.shard_map(
        per_device,
        mesh=mesh,
        in_specs=(P(("row", "col"), None, None, None), P()),
        out_specs=P(("row", "col"), None, None, None),
        check_vma=False,
    )
```

profile of v0, /device:TPU:1, one launch (start us, length us, event | category | flops | bytes accessed | tf_op | source)
XLA Modules:
  0.0 403.7 jit_solution(2100939602717630604)
XLA Ops:
  8.6 2.2 collective-permute-start
  10.7 5.0 %collective-permute-start.1 = (f32[1,2,4,128,128]{3,4,1,2,0:T(8,128)S(1)}, f32[1,2,4,128,128]{3,4,1,2,0:T(8,128)}, u32[]{:S(2)}, u32[]{:S(2)}) collective-permute-start(f32[1,2,4,128,128]{3,4,1,2,0:T(8,128)S(1)} %bitcast.234), channel_id=1, source_target_pairs={{1,0},{2,1},{3,2},{4,3},{5,4},{6,5},{7,6},{8,7},{9,8},{10,9},{11,1... | collective-permute-start | bytes 1572872 | tf_op jit(solution)/shard_map/ppermute | solution.py:22
  22.9 4.3 %collective-permute-done = f32[1,2,4,128,128]{3,4,1,2,0:T(8,128)S(1)} collective-permute-done((f32[1,2,4,128,128]{3,4,1,2,0:T(8,128)S(1)}, f32[1,2,4,128,128]{3,4,1,2,0:T(8,128)S(1)}, u32[]{:S(2)}, u32[]{:S(2)}) %collective-permute-start) | collective-permute-done | bytes 524320 | tf_op jit(solution)/shard_map/ppermute | solution.py:19
  29.8 14.9 %all-gather.7.cloned.1.call-done = f32[16,4,128,128]{3,2,1,0:T(8,128)} async-done(((f32[2,4,128,128]{3,2,1,0:T(8,128)}), f32[16,4,128,128]{3,2,1,0:T(8,128)}) %all-gather.7.cloned.1.call-update) | async-done | bytes 4194320 | tf_op jit(solution)/shard_map/all_gather | solution.py:78
  44.7 2.8 gather_fusion
  57.9 2.0 copy.152
  59.9 2.1 fusion.77
  63.0 2.2 select_dynamic-update-slice_fusion.2
  66.9 2.8 select_dynamic-update-slice_fusion.1
  71.7 2.9 fusion.91
  77.4 2.1 reshape.911
  79.5 4.8 %multiply_reduce_fusion.1 = (f32[2]{0:T(128)S(1)}, f32[2,512,512]{2,1,0:T(8,128)}) fusion(f32[2,512,512]{2,1,0:T(8,128)S(1)} %reshape.911), kind=kOutput, calls=%fused_computation.38 | convolution fusion | flops 3222274048 | bytes 4194312 | tf_op jit(solution)/shard_map/sab,sbc->sac/dot_general | solution.py:91
  85.6 65.2 %pmax.14 = f32[]{:T(128)} all-reduce(f32[]{:T(128)} %reduce_max.18), channel_id=1, replica_groups=mesh['row'=8,'col'=16] {'row','col'}, use_global_device_ids=true, to_apply=%region_5.6 | all-reduce | flops 1 | bytes 8 | tf_op jit(solution)/shard_map/pmax | solution.py:95
  151.5 5.3 %fusion.29 = f32[2,512,512]{2,1,0:T(8,128)S(1)} fusion(f32[2,512,512]{2,1,0:T(8,128)} %get-tuple-element.289, f32[2,512,512]{2,1,0:T(8,128)S(1)} %reshape.911, f32[]{:T(128)S(6)} %mul.227, f32[512,512]{1,0:T(8,128)S(1)} %broadcast_select_fusion, f32[]{:T(128)S(6)} %div.33), kind=kOutput, calls=%fused_computation.33 | convolution fusion | flops 3223322624 | bytes 7340040 | tf_op jit(solution)/shard_map/sab,sbc->sac/dot_general | solution.py:56
  156.9 3.5 fusion.125
  160.4 3.7 fusion.26
  164.1 3.7 fusion.126
  167.9 3.7 fusion.23
  171.6 3.5 fusion.127
  175.1 3.7 fusion.20
  178.8 3.8 fusion.128
  182.6 3.7 fusion.17
  186.3 3.5 fusion.129
  189.8 1.9 fusion.35
  194.0 4.1 %collective-permute-start.3 = (f32[1,2,4,128,128]{3,4,1,2,0:T(8,128)S(1)}, f32[1,2,4,128,128]{3,4,1,2,0:T(8,128)}, u32[]{:S(2)}, u32[]{:S(2)}) collective-permute-start(f32[1,2,4,128,128]{3,4,1,2,0:T(8,128)S(1)} %broadcast_multiply_fusion.1), channel_id=1, source_target_pairs={{1,0},{2,1},{3,2},{4,3},{5,4},{6,5},{7,6},{8,7},{9,8},{10,9},{11,1... | collective-permute-start | bytes 1572872 | tf_op jit(solution)/shard_map/ppermute | solution.py:22
  199.0 10.6 %collective-permute-done.2 = f32[1,2,4,128,128]{3,4,1,2,0:T(8,128)} collective-permute-done((f32[1,2,4,128,128]{3,4,1,2,0:T(8,128)S(1)}, f32[1,2,4,128,128]{3,4,1,2,0:T(8,128)}, u32[]{:S(2)}, u32[]{:S(2)}) %collective-permute-start.2) | collective-permute-done | bytes 524320 | tf_op jit(solution)/shard_map/ppermute | solution.py:19
  216.4 3.3 copy.160
  219.6 2.2 gather_fusion.1
  237.0 2.2 select_dynamic-update-slice_fusion
  246.6 3.6 fusion.89
  251.8 4.2 %copy.187 = f32[2,4,128,4,128]{4,3,2,1,0:T(4,128)} copy(f32[2,4,128,4,128]{4,2,0,3,1:T(8,128)} %fusion.82) | data formatting | bytes 4194304 | tf_op jit(solution)/shard_map/vmap()/scatter | solution.py:41
  256.0 2.1 reshape.924
  258.1 4.8 %multiply_reduce_fusion = (f32[2]{0:T(128)S(1)}, f32[2,512,512]{2,1,0:T(8,128)}) fusion(f32[2,512,512]{2,1,0:T(8,128)S(1)} %reshape.924), kind=kOutput, calls=%fused_computation.20 | convolution fusion | flops 3222274048 | bytes 4194312 | tf_op jit(solution)/shard_map/sab,sbc->sac/dot_general | solution.py:91
  263.5 64.8 %pmax.15 = f32[]{:T(128)} all-reduce(f32[]{:T(128)} %reduce_max.19), channel_id=1, replica_groups=mesh['row'=8,'col'=16] {'row','col'}, use_global_device_ids=true, to_apply=%region_8.9 | all-reduce | flops 1 | bytes 8 | tf_op jit(solution)/shard_map/pmax | solution.py:95
  329.1 5.3 %fusion.12 = f32[2,512,512]{2,1,0:T(8,128)S(1)} fusion(f32[2,512,512]{2,1,0:T(8,128)} %get-tuple-element.291, f32[2,512,512]{2,1,0:T(8,128)S(1)} %reshape.924, f32[]{:T(128)S(6)} %mul.251, f32[]{:T(128)S(6)} %div.34, f32[512,512]{1,0:T(8,128)S(1)} %broadcast_select_fusion), kind=kOutput, calls=%fused_computation.15 | convolution fusion | flops 3223322624 | bytes 7340040 | tf_op jit(solution)/shard_map/sab,sbc->sac/dot_general | solution.py:56
  334.4 3.5 fusion.130
  338.0 3.7 fusion.9
  341.7 3.8 fusion.131
  345.5 3.7 fusion.6
  349.2 3.5 fusion.132
  352.7 3.7 fusion.3
  356.4 3.8 fusion.133
  360.2 3.7 fusion
  363.9 3.5 fusion.134
  367.5 1.9 fusion.34
  371.2 4.5 %collective-permute-start.5 = (f32[1,2,4,128,128]{3,4,1,2,0:T(8,128)S(1)}, f32[1,2,4,128,128]{3,4,1,2,0:T(8,128)S(1)}, u32[]{:S(2)}, u32[]{:S(2)}) collective-permute-start(f32[1,2,4,128,128]{3,4,1,2,0:T(8,128)S(1)} %broadcast_multiply_fusion), channel_id=1, source_target_pairs={{1,0},{2,1},{3,2},{4,3},{5,4},{6,5},{7,6},{8,7},{9,8},{10,9},{11,1... | collective-permute-start | bytes 1572872 | tf_op jit(solution)/shard_map/ppermute | solution.py:22
  375.9 11.2 %collective-permute-done.4 = f32[1,2,4,128,128]{3,4,1,2,0:T(8,128)S(1)} collective-permute-done((f32[1,2,4,128,128]{3,4,1,2,0:T(8,128)S(1)}, f32[1,2,4,128,128]{3,4,1,2,0:T(8,128)S(1)}, u32[]{:S(2)}, u32[]{:S(2)}) %collective-permute-start.4) | collective-permute-done | bytes 524320 | tf_op jit(solution)/shard_map/ppermute | solution.py:19
  387.1 6.1 %all-gather.11.cloned.1.call-done = f32[16,2,128,128]{2,3,0,1:T(8,128)} async-done(((f32[2,2,128,128]{2,3,0,1:T(8,128)}), f32[16,2,128,128]{2,3,0,1:T(8,128)}) %all-gather.11.cloned.1.call-update) | async-done | bytes 2097168 | tf_op jit(solution)/shard_map/all_gather | solution.py:104
  (157 shorter events, 70.5 us)
Async XLA Ops:
  6.5 15.7 %copy-start.17 = (s32[5]{0:T(128)S(1)}, s32[5]{0:T(128)}, u32[]{:S(2)}) copy-start(s32[5]{0:T(128)} %constant.550.clone.1) | copy-start | bytes 64
  6.5 38.2 %all-gather.7.cloned.1.call-start = ((), (), s32[]{:S(2)}) async-start(), calls=%async_computation | async-start | bytes 4718592 | tf_op jit(solution)/shard_map/all_gather | solution.py:78
  7.3 209.1 %all-gather.9.cloned.1.call-start = ((), (), s32[]{:S(2)}) async-start(), calls=%async_computation.1 | async-start | bytes 2359296 | tf_op jit(solution)/shard_map/all_gather | solution.py:104
  8.6 18.7 %collective-permute-start = (f32[1,2,4,128,128]{3,4,1,2,0:T(8,128)S(1)}, f32[1,2,4,128,128]{3,4,1,2,0:T(8,128)S(1)}, u32[]{:S(2)}, u32[]{:S(2)}) collective-permute-start(f32[1,2,4,128,128]{3,4,1,2,0:T(8,128)S(1)} %bitcast.233), channel_id=1, source_target_pairs={{0,1},{1,2},{2,3},{3,4},{4,5},{5,6},{6,7},{7,8},{8,9},{9,10},{10,1... | collective-permute-start | bytes 1572872 | tf_op jit(solution)/shard_map/ppermute | solution.py:19
  10.7 17.3 %collective-permute-start.1 = (f32[1,2,4,128,128]{3,4,1,2,0:T(8,128)S(1)}, f32[1,2,4,128,128]{3,4,1,2,0:T(8,128)}, u32[]{:S(2)}, u32[]{:S(2)}) collective-permute-start(f32[1,2,4,128,128]{3,4,1,2,0:T(8,128)S(1)} %bitcast.234), channel_id=1, source_target_pairs={{1,0},{2,1},{3,2},{4,3},{5,4},{6,5},{7,6},{8,7},{9,8},{10,9},{11,1... | collective-permute-start | bytes 1572872 | tf_op jit(solution)/shard_map/ppermute | solution.py:22
  22.1 26.3 %copy-start = (f32[2,4,128,128]{3,2,1,0:T(8,128)S(1)}, f32[2,4,128,128]{3,2,1,0:T(8,128)}, u32[]{:S(2)}) copy-start(f32[2,4,128,128]{3,2,1,0:T(8,128)} %param.42) | copy-start | bytes 1572868
  27.3 0.9 copy-start.14
  47.5 4.0 %copy-start.7 = (f32[2,4,128,128]{3,2,1,0:T(8,128)}, f32[2,4,128,128]{3,2,1,0:T(8,128)S(1)}, u32[]{:S(2)}) copy-start(f32[2,4,128,128]{3,2,1,0:T(8,128)S(1)} %gather_fusion) | copy-start | bytes 1572868
  48.4 0.8 copy-start.3
  51.5 1.2 copy-start.10
  186.3 3.6 copy-start.4
  192.9 200.3 %all-gather.11.cloned.1.call-start = ((), (), s32[]{:S(2)}) async-start(), calls=%async_computation.2 | async-start | bytes 2359296 | tf_op jit(solution)/shard_map/all_gather | solution.py:104
  193.2 16.3 %collective-permute-start.2 = (f32[1,2,4,128,128]{3,4,1,2,0:T(8,128)S(1)}, f32[1,2,4,128,128]{3,4,1,2,0:T(8,128)}, u32[]{:S(2)}, u32[]{:S(2)}) collective-permute-start(f32[1,2,4,128,128]{3,4,1,2,0:T(8,128)S(1)} %broadcast_multiply_fusion.1), channel_id=1, source_target_pairs={{0,1},{1,2},{2,3},{3,4},{4,5},{5,6},{6,7},{7,8},{8,9},{9,10},{10,1... | collective-permute-start | bytes 1572872 | tf_op jit(solution)/shard_map/ppermute | solution.py:19
  194.0 17.3 %collective-permute-start.3 = (f32[1,2,4,128,128]{3,4,1,2,0:T(8,128)S(1)}, f32[1,2,4,128,128]{3,4,1,2,0:T(8,128)}, u32[]{:S(2)}, u32[]{:S(2)}) collective-permute-start(f32[1,2,4,128,128]{3,4,1,2,0:T(8,128)S(1)} %broadcast_multiply_fusion.1), channel_id=1, source_target_pairs={{1,0},{2,1},{3,2},{4,3},{5,4},{6,5},{7,6},{8,7},{9,8},{10,9},{11,1... | collective-permute-start | bytes 1572872 | tf_op jit(solution)/shard_map/ppermute | solution.py:22
  216.4 6.2 %copy-start.1 = (f32[2,4,128,128]{3,2,1,0:T(8,128)S(1)}, f32[2,4,128,128]{3,2,1,0:T(8,128)}, u32[]{:S(2)}) copy-start(f32[2,4,128,128]{3,2,1,0:T(8,128)} %param.42) | copy-start | bytes 1572868
  222.6 3.8 copy-start.6
  224.5 2.6 copy-start.11
  224.5 2.6 copy-start.12
  226.4 0.7 copy-start.13
  227.3 3.0 copy-start.9
  228.7 3.9 copy-start.15
  228.8 4.5 %copy-start.8 = (f32[2,4,128,128]{3,2,0,1:T(8,128)}, f32[2,4,128,128]{3,2,0,1:T(8,128)S(1)}, u32[]{:S(2)}) copy-start(f32[2,4,128,128]{3,2,0,1:T(8,128)S(1)} %broadcast_multiply_fusion.4) | copy-start | bytes 1572868
  233.4 1.1 copy-start.2
  244.0 1.8 copy-start.16
  363.9 3.6 copy-start.5
  370.8 16.2 %collective-permute-start.4 = (f32[1,2,4,128,128]{3,4,1,2,0:T(8,128)S(1)}, f32[1,2,4,128,128]{3,4,1,2,0:T(8,128)S(1)}, u32[]{:S(2)}, u32[]{:S(2)}) collective-permute-start(f32[1,2,4,128,128]{3,4,1,2,0:T(8,128)S(1)} %broadcast_multiply_fusion), channel_id=1, source_target_pairs={{0,1},{1,2},{2,3},{3,4},{4,5},{5,6},{6,7},{7,8},{8,9},{9,10},{10,1... | collective-permute-start | bytes 1572872 | tf_op jit(solution)/shard_map/ppermute | solution.py:19
  371.2 15.9 %collective-permute-start.5 = (f32[1,2,4,128,128]{3,4,1,2,0:T(8,128)S(1)}, f32[1,2,4,128,128]{3,4,1,2,0:T(8,128)S(1)}, u32[]{:S(2)}, u32[]{:S(2)}) collective-permute-start(f32[1,2,4,128,128]{3,4,1,2,0:T(8,128)S(1)} %broadcast_multiply_fusion), channel_id=1, source_target_pairs={{1,0},{2,1},{3,2},{4,3},{5,4},{6,5},{7,6},{8,7},{9,8},{10,9},{11,1... | collective-permute-start | bytes 1572872 | tf_op jit(solution)/shard_map/ppermute | solution.py:22
Sparse Core Ops, SparseCore 0:
  9.0 35.6 all-gather.6
  193.0 22.8 all-gather.8
  370.7 22.4 all-gather.10
where the time goes:
time: 411 us; the launch traced here: 404 us
  blocking collectives  130 us (32%)
  matrix products  90.1 us (22%)
  local copies, waits for them, and re-layouts  69.1 us (17%)
  waiting for transfers between devices  47.9 us (12%)
  other arithmetic  33.9 us (8%)
  starting transfers between devices  17 us (4%)
  between operations  15.9 us (4%)
    pmax x2, blocking collectives, per_device(): largest = lax.pmax(local_top, ('row', 'col'))  130 us
    dot_general x12, matrix products, sign_batch(): jnp.einsum('sab,sbc->sac', iterate, 1.5 * identity - 0.5 * square, precis...  44.1 us
    dot_general x10, matrix products, sign_batch(): jnp.einsum('sab,sbc->sac', iterate, iterate, precision=lax.Precision.HIGH...  36.3 us
    ppermute x3, waiting for transfers between devices, with_halo(): lax.ppermute(lax.slice_in_dim(block, block.shape[dim] - width, None, axis...  26.1 us
    scatter x6, other arithmetic, assemble(): matrix = matrix.at[0, :, position, :].set(column[position].T)  15.7 us
    all_gather x1, waiting for transfers between devices, per_device(): everyone = lax.all_gather(hamiltonian[None], 'row', axis=0, tiled=True)  14.9 us
    another operation x17, local copies, waits for them, and re-layouts  13.6 us
    ppermute x3, starting transfers between devices, with_halo(): lax.ppermute(lax.slice_in_dim(block, 0, width, axis=dim), axis, backward)  13.5 us
  transfers between devices with their start and end apart: 9, of which 5 were waited for; matrix products, arithmetic and copies ran while one was open for 5% of the time, Pallas kernels for 0%

commit v1 on v0

v1 whole, which is shorter than its diff:
```python
import jax
import jax.numpy as jnp
from jax import lax
from jax.experimental import pallas as pl
from jax.experimental.pallas import tpu as pltpu
from jax.sharding import PartitionSpec as P

STEPS = 2
SLOTS = 2
B = 128
N = 512
T = 256
EPS = 1e-06
ROWS = 8
COLS = 16
f32 = jnp.float32
bf16 = jnp.bfloat16
MESH = pl.DeviceIdType.MESH


def dot(a, b):
    return jnp.dot(a, b, preferred_element_type=f32)


def put(ref, r, c, x):
    m, n = x.shape
    h = x.astype(bf16)
    ref[r : r + m, c : c + n] = h
    ref[r : r + m, N + c : N + c + n] = (x - h.astype(f32)).astype(bf16)


def put_symmetric(ref, f):
    put(ref, 0, 0, f[:T, :T])
    upper = f[:T, T:]
    put(ref, 0, T, upper)
    put(ref, T, 0, upper.T)
    put(ref, T, T, f[T:, T:])


def square(x, q, low):
    low[...] = dot(x[:, :N], x[:, N:])
    a = dot(x[:T, :N], x[:, :T])
    t00 = a + low[:T, :T] + low[:T, :T].T
    put(q, 0, 0, t00)
    a = dot(x[:, :N], x[:, T:N])
    t01 = a[:T] + low[:T, T:] + low[T:, :T].T
    put(q, 0, T, t01)
    put(q, T, 0, t01.T)
    t11 = a[T:] + low[T:, T:] + low[T:, T:].T
    put(q, T, T, t11)
    return t00, t01, t11


def product(x, q, store):
    for m, c in ((T, 0), (N, T)):
        h, l = x[:m, :N], x[:m, N:]
        qh, ql = q[:, c : c + T], q[:, N + c : N + c + T]
        store(m, c, dot(jnp.concatenate([h, h, l], 1), jnp.concatenate([qh, ql, qh], 0)))


def rowmul(v, q):
    h = v.astype(bf16)
    l = (v - h.astype(f32)).astype(bf16)
    p = dot(jnp.concatenate([h, l], 0), q[:, :N])
    return p[:B] + p[B:] + dot(h, q[:, N:])


def kernel(
    lists, h_any, out, hv, rb0, rb1, rb2, sm, fm, x0, q0, l0, x1, q1, l1, dct, dg, own1, own2, mx1, mx2,
    hsem, es, er, ms, mr,
):
    row, col = lax.axis_index("row"), lax.axis_index("col")
    rb = (rb0, rb1, rb2)
    xs, qs, ls = (x0, x1), (q0, q1), (l0, l1)
    row_c = row + 1 - 2 * (row % 2)
    row_x = row + 2 - 4 * ((row // 2) % 2)
    row_f = (row_x + 4) % ROWS

    load = pltpu.make_async_copy(h_any, hv, hsem)
    load.start()
    barrier = pltpu.get_barrier_semaphore()
    for d in range(1, ROWS):
        pl.semaphore_signal(barrier, inc=1, device_id=((row + d) % ROWS, col), device_id_type=MESH)
    for d in range(1, COLS):
        pl.semaphore_signal(barrier, inc=1, device_id=(row, (col + d) % COLS), device_id_type=MESH)

    def cp(e, d, s, q):
        target = (
            (row, (col + 1) % COLS),
            (row, (col + COLS - 1) % COLS),
            (row_c, col),
            (row_x, col),
            (row_f, col),
        )[d]
        face = (2, 1, 3, 3, 3)[d]
        if d == 4:
            src = rb[e].at[3, s, q]
        elif e == 0:
            src = hv.at[s, face if q else 0]
        elif e == 1:
            src = dct.at[0, s, face] if q else dg.at[0, s]
        else:
            src = dct.at[1, s, face, pl.ds(64 * q, 64)]
        return pltpu.make_async_remote_copy(
            src_ref=src,
            dst_ref=rb[e].at[d, s, q],
            send_sem=es.at[e, d, s, q],
            recv_sem=er.at[e, d, s, q],
            device_id=target,
            device_id_type=MESH,
        )

    def send(e, s):
        for q in range(2):
            for d in (3, 0, 1, 2):
                cp(e, d, s, q).start()

    def relay(e, s):
        for q in range(2):
            cp(e, 3, s, q).wait_recv()
            cp(e, 4, s, q).start()

    def arrived(e, s, dirs):
        for d in dirs:
            for q in range(2):
                cp(e, d, s, q).wait_recv()

    def maxcp(t, k):
        if k < ROWS:
            src, dst, target = own1.at[t], mx1.at[t, k], ((row + k) % ROWS, col)
        else:
            d = k - ROWS + 1
            src, dst, target = own2.at[t], mx2.at[t, d], (row, (col + d) % COLS)
        return pltpu.make_async_remote_copy(
            src_ref=src, dst_ref=dst, send_sem=ms.at[t, k], recv_sem=mr.at[t, k], device_id=target, device_id_type=MESH
        )

    present, chosen = [], []
    for s in range(SLOTS):
        j = (row * COLS + col) * SLOTS + s
        present.append([1.0] + [jnp.where(lists[j, k] >= 0, 1.0, 0.0).astype(f32) for k in range(1, 4)])
        apart = jnp.abs(lists[j, 3] // (SLOTS * COLS) - row)
        chosen.append((apart < 2, apart < 4))

    def got(e, s, k, q):
        if k < 3:
            return rb[e][k - 1, s, q]
        near, mid = chosen[s]
        return jnp.where(near, rb[e][2, s, q], jnp.where(mid, rb[e][3, s, q], rb[e][4, s, q]))

    blk = [slice(B * k, B * k + B) for k in range(4)]

    def assemble(t, s):
        x = xs[s]
        if t == 0:
            h = hv[s, 0]
            d = 0.5 * (h + h.T)
        else:
            d = sm[s, blk[0], blk[0]] + dg[0, s]
        sm[s, blk[0], blk[0]] = d
        put(x, 0, 0, d)
        for k in range(1, 4):
            p = present[s][k]
            diag, face = got(t, s, k, 0), got(t, s, k, 1)
            if t == 0:
                low = (0.5 * p) * (hv[s, k] + face.T)
                d = (0.5 * p) * (diag + diag.T)
            else:
                low = sm[s, blk[k], blk[0]] + (0.5 * p) * (dct[0, s, k].T + face)
                d = sm[s, blk[k], blk[k]] + p * diag
            up = low.T
            sm[s, blk[k], blk[0]] = low
            sm[s, blk[0], blk[k]] = up
            sm[s, blk[k], blk[k]] = d
            put(x, B * k, 0, low)
            put(x, 0, B * k, up)
            put(x, B * k, B * k, d)
            for i in range(1, 4):
                if t != 0 and i != k:
                    put(x, B * k, B * i, jnp.zeros((B, B), f32))

    def combine(s, alpha, beta):
        for r, c in ((0, 0), (0, T), (T, T)):
            f = alpha * sm[s, r : r + T, c : c + T] - beta * fm[s, r : r + T, c : c + T]
            fm[s, r : r + T, c : c + T] = f
            put(xs[s], r, c, f)
            if r != c:
                put(xs[s], c, r, f.T)

    def cube(s):
        def store(m, c, p):
            fm[s, :m, c : c + T] = p

        product(xs[s], qs[s], store)

    def advance(s):
        def store(m, c, p):
            fm[s, :m, c : c + T] = 1.5 * fm[s, :m, c : c + T] - 0.5 * p

        product(xs[s], qs[s], store)
        put_symmetric(xs[s], fm[s])

    def sq(s):
        return square(xs[s], qs[s], ls[s])

    def norm(s):
        t00, t01, t11 = sq(s)
        total = t00 * t00 + 2.0 * (t01 * t01) + t11 * t11
        return jnp.sum(total, axis=(0, 1), keepdims=True)

    def tail(t, s):
        y = qs[s]
        v = fm[s, :B, :]
        w = 1.5 * v - 0.5 * rowmul(v, y)
        a = rowmul(w, y)
        a = 1.5 * a - 0.5 * rowmul(a, y)
        a = 1.5 * a - 0.5 * rowmul(a, y)
        z = 1.5 * w - 0.5 * a
        eye = (lax.broadcasted_iota(jnp.int32, (B, B), 0) == lax.broadcasted_iota(jnp.int32, (B, B), 1)).astype(f32)
        centre = 0.5 * (eye - z[:, blk[0]])
        dg[t, s] = 0.5 * (centre + centre.T)
        for k in range(1, 4):
            dct[t, s, k] = (-0.5 * present[s][k]) * z[:, blk[k]]

    for x in xs:
        x[...] = jnp.zeros_like(x)
    sm[...] = jnp.zeros_like(sm)
    load.wait()
    pl.semaphore_wait(barrier, ROWS + COLS - 2)

    for s in range(SLOTS):
        send(0, s)
    for s in range(SLOTS):
        relay(0, s)

    for t in range(STEPS):
        arrived(t, 0, (0, 1, 2, 4))
        assemble(t, 0)
        n0 = norm(0)
        if t == 1:
            relay(1, 1)
        arrived(t, 1, (0, 1, 2, 4))
        assemble(t, 1)
        n1 = norm(1)
        own1[t] = jnp.broadcast_to(jnp.maximum(n0, n1), (8, 128))
        for k in range(1, ROWS):
            maxcp(t, k).start()
        cube(0)
        for k in range(1, ROWS):
            maxcp(t, k).wait_recv()
        top = own1[t]
        for k in range(1, ROWS):
            top = jnp.maximum(top, mx1[t, k])
        own2[t] = top
        for k in range(ROWS, ROWS + COLS - 1):
            maxcp(t, k).start()
        cube(1)
        for k in range(ROWS, ROWS + COLS - 1):
            maxcp(t, k).wait_recv()
            top = jnp.maximum(top, mx2[t, k - ROWS + 1])
        scale = 1.5 / jnp.sqrt(jnp.sqrt(top + EPS))
        alpha = (1.5 * scale)[:1, :1]
        beta = (0.5 * scale * scale * scale)[:1, :1]
        combine(0, alpha, beta)
        combine(1, alpha, beta)
        sq(0)

        def body(i, carry):
            advance(0)
            sq(1)
            sq(0)
            advance(1)
            return carry

        lax.fori_loop(0, 3, body, 0)
        tail(t, 0)
        send(t + 1, 0)
        sq(1)
        tail(t, 1)
        send(t + 1, 1)
        relay(t + 1, 0)

    def finish(s):
        arrived(2, s, (0, 1, 2, 4))
        out[s, 0] = dg[1, s]
        for k in range(1, 4):
            face = jnp.concatenate([got(2, s, k, 0), got(2, s, k, 1)], 0)
            out[s, k] = (0.5 * present[s][k]) * (dct[1, s, k].T + face)

    relay(2, 1)
    for s in range(SLOTS):
        finish(s)

    for e in range(STEPS + 1):
        for s in range(SLOTS):
            for d in range(5):
                for q in range(2):
                    cp(e, d, s, q).wait_send()
    for t in range(STEPS):
        for k in range(1, ROWS + COLS - 1):
            maxcp(t, k).wait_send()


def per_device(hamiltonian, block_lists):
    mat = pltpu.VMEM((N, N), f32)
    halves = pltpu.VMEM((N, 2 * N), bf16)
    return pl.pallas_call(
        kernel,
        out_shape=jax.ShapeDtypeStruct((SLOTS, 4, B, B), f32),
        in_specs=[pl.BlockSpec(memory_space=pltpu.SMEM), pl.BlockSpec(memory_space=pl.ANY)],
        out_specs=pl.BlockSpec(memory_space=pltpu.VMEM),
        scratch_shapes=[
            pltpu.VMEM((SLOTS, 4, B, B), f32),
            pltpu.VMEM((5, SLOTS, 2, B, B), f32),
            pltpu.VMEM((5, SLOTS, 2, B, B), f32),
            pltpu.VMEM((5, SLOTS, 2, B // 2, B), f32),
            pltpu.VMEM((SLOTS, N, N), f32),
            pltpu.VMEM((SLOTS, N, N), f32),
            halves, halves, mat,
            halves, halves, mat,
            pltpu.VMEM((STEPS, SLOTS, 4, B, B), f32),
            pltpu.VMEM((STEPS, SLOTS, B, B), f32),
            pltpu.VMEM((STEPS, 8, 128), f32),
            pltpu.VMEM((STEPS, 8, 128), f32),
            pltpu.VMEM((STEPS, ROWS, 8, 128), f32),
            pltpu.VMEM((STEPS, COLS, 8, 128), f32),
            pltpu.SemaphoreType.DMA,
            pltpu.SemaphoreType.DMA((3, 5, SLOTS, 2)),
            pltpu.SemaphoreType.DMA((3, 5, SLOTS, 2)),
            pltpu.SemaphoreType.DMA((STEPS, ROWS + COLS - 1)),
            pltpu.SemaphoreType.DMA((STEPS, ROWS + COLS - 1)),
        ],
        compiler_params=pltpu.CompilerParams(collective_id=0, has_side_effects=True),
    )(block_lists, hamiltonian)


def solution(mesh):
    return jax.shard_map(
        per_device,
        mesh=mesh,
        in_specs=(P(("row", "col"), None, None, None), P()),
        out_specs=P(("row", "col"), None, None, None),
        check_vma=False,
    )
```

time: 411 us -> 91.4 us (0.22); the launches traced: 404 us -> 90.3 us
  blocking collectives: 130 us -> 0 us
  matrix products: 90.1 us -> 0 us
  Pallas kernels: 0 us -> 86.9 us
  local copies, waits for them, and re-layouts: 69.1 us -> 3.35 us
  waiting for transfers between devices: 47.9 us -> 0 us
  other arithmetic: 33.9 us -> 0 us
  starting transfers between devices: 17 us -> 0 us
  between operations: 15.9 us -> 0.01 us
    pmax x2 -> x0, blocking collectives: 130 us -> none  [per_device(): largest = lax.pmax(local_top, ('row', 'col'))]
    dot_general x24 -> x0, matrix products: 90.1 us -> none  [the longest x12 44.1 us: sign_batch(): jnp.einsum('sab,sbc->sac', iterate, 1.5 * identity - 0.5 * square, precis...]
    pallas_call x0 -> x1, Pallas kernels: none -> 86.9 us  [per_device(): pl.pallas_call(kernel, out_shape=jax.ShapeDtypeStruct((SLOTS, 4, B, B), f...]
    ppermute x6 -> x0, waiting for transfers between devices: 26.1 us -> none  [the longest x3 26.1 us: with_halo(): lax.ppermute(lax.slice_in_dim(block, block.shape[dim] - width, None, axis...]
    all_gather x3 -> x0, waiting for transfers between devices: 21 us -> none  [the longest x1 14.9 us: per_device(): everyone = lax.all_gather(hamiltonian[None], 'row', axis=0, tiled=True)]
    ppermute x6 -> x0, starting transfers between devices: 16.9 us -> none  [the longest x3 13.5 us: with_halo(): lax.ppermute(lax.slice_in_dim(block, 0, width, axis=dim), axis, backward)]
    scatter x17 -> x0, local copies, waits for them, and re-layouts: 16.2 us -> none  [the longest x9 13.1 us: assemble(): matrix = matrix.at[position, :, position, :].set(blocks[position])]
    another operation x19 -> x0, local copies, waits for them, and re-layouts: 15.8 us -> none
  transfers between devices with their start and end apart: 9 -> 0, of which waited for: 5 -> 0; matrix products, arithmetic and copies ran while one was open for 5% -> 0% of each run, Pallas kernels for 0% -> 0%
where the time goes in v1:
time: 91.4 us; the launch traced here: 90.3 us
  Pallas kernels  86.9 us (95%)
  local copies, waits for them, and re-layouts  3.35 us (4%)
    pallas_call x1, Pallas kernels, per_device(): pl.pallas_call(kernel, out_shape=jax.ShapeDtypeStruct((SLOTS, 4, B, B), f...  86.9 us
    unnamed x2, local copies, waits for them, and re-layouts  3.35 us

profile of v1, /device:TPU:1, one launch (start us, length us, event | category | flops | bytes accessed | tf_op | source)
XLA Modules:
  0.0 90.3 jit_solution(14943176290506957385)
XLA Ops:
  0.0 1.5 %copy.3.lists = s32[256,4]{1,0:T(8,128)} copy(s32[256,4]{0,1:T(4,128)} %param.3) | data formatting | bytes 8192 | tf_op args[1]
  1.5 86.9 %shard_map.28 = f32[2,4,128,128]{3,2,1,0:T(8,128)} custom-call(s32[256,4]{1,0:T(8,128)} %copy.3.lists, f32[2,4,128,128]{3,2,1,0:T(8,128)} %h_any.1), custom_call_target="tpu_custom_call" | custom-call | tf_op jit(solution)/shard_map/pallas_call | solution.py:307
  88.4 1.9 %copy.5 = f32[2,4,128,128]{3,2,1,0:T(8,128)} copy(f32[2,4,128,128]{3,2,1,0:T(8,128)} %shard_map.28) | data formatting | bytes 1048576

commit v2 on v1

--- a/solution.py
+++ b/solution.py
@@ -66,23 +66,36 @@
 
 
 def kernel(
-    lists, h_any, out, hv, rb0, rb1, rb2, sm, fm, x0, q0, l0, x1, q1, l1, dct, dg, own1, own2, mx1, mx2,
+    lists, h_any, out, hv, rb0, rb1, rb2, sm, fm, pw, x0, q0, l0, c0, d0, e0, x1, q1, l1, c1, d1, e1, dct, dg, own1, own2, mx1, mx2,
     hsem, es, er, ms, mr,
 ):
     row, col = lax.axis_index("row"), lax.axis_index("col")
     rb = (rb0, rb1, rb2)
     xs, qs, ls = (x0, x1), (q0, q1), (l0, l1)
+    thirds, fourths, fifths = (c0, c1), (d0, d1), (e0, e1)
     row_c = row + 1 - 2 * (row % 2)
     row_x = row + 2 - 4 * ((row // 2) % 2)
     row_f = (row_x + 4) % ROWS
 
+    def row_peer(k):
+        return (2 * ((row // 2 + k // 2) % 4) + (row % 2 + k % 2) % 2, col)
+
+    def col_peer(k):
+        return (row, 4 * ((col // 4 + k // 4) % 4) + (col % 4 + k % 4) % 4)
+
+    def hops(n):
+        return min(n, 4 - n)
+
+    row_order = sorted(range(1, ROWS), key=lambda k: -hops(k // 2) - k % 2 / 4)
+    col_order = [ROWS + k for k in sorted(range(1, COLS), key=lambda k: -hops(k // 4) - hops(k % 4))]
+
     load = pltpu.make_async_copy(h_any, hv, hsem)
     load.start()
     barrier = pltpu.get_barrier_semaphore()
-    for d in range(1, ROWS):
-        pl.semaphore_signal(barrier, inc=1, device_id=((row + d) % ROWS, col), device_id_type=MESH)
-    for d in range(1, COLS):
-        pl.semaphore_signal(barrier, inc=1, device_id=(row, (col + d) % COLS), device_id_type=MESH)
+    for k in col_order:
+        pl.semaphore_signal(barrier, inc=1, device_id=col_peer(k - ROWS), device_id_type=MESH)
+    for k in row_order:
+        pl.semaphore_signal(barrier, inc=1, device_id=row_peer(k), device_id_type=MESH)
 
     def cp(e, d, s, q):
         target = (
@@ -125,12 +138,17 @@
             for q in range(2):
                 cp(e, d, s, q).wait_recv()
 
+    def sent(e):
+        for s in range(SLOTS):
+            for d in range(5):
+                for q in range(2):
+                    cp(e, d, s, q).wait_send()
+
     def maxcp(t, k):
         if k < ROWS:
-            src, dst, target = own1.at[t], mx1.at[t, k], ((row + k) % ROWS, col)
+            src, dst, target = own1.at[t], mx1.at[t, k], row_peer(k)
         else:
-            d = k - ROWS + 1
-            src, dst, target = own2.at[t], mx2.at[t, d], (row, (col + d) % COLS)
+            src, dst, target = own2.at[t], mx2.at[t, k - ROWS], col_peer(k - ROWS)
         return pltpu.make_async_remote_copy(
             src_ref=src, dst_ref=dst, send_sem=ms.at[t, k], recv_sem=mr.at[t, k], device_id=target, device_id_type=MESH
         )
@@ -138,8 +156,8 @@
     present, chosen = [], []
     for s in range(SLOTS):
         j = (row * COLS + col) * SLOTS + s
-        present.append([1.0] + [jnp.where(lists[j, k] >= 0, 1.0, 0.0).astype(f32) for k in range(1, 4)])
-        apart = jnp.abs(lists[j, 3] // (SLOTS * COLS) - row)
+        present.append([1.0] + [jnp.where(lists[k, j] >= 0, 1.0, 0.0).astype(f32) for k in range(1, 4)])
+        apart = jnp.abs(lists[3, j] // (SLOTS * COLS) - row)
         chosen.append((apart < 2, apart < 4))
 
     def got(e, s, k, q):
@@ -179,19 +197,45 @@
                 if t != 0 and i != k:
                     put(x, B * k, B * i, jnp.zeros((B, B), f32))
 
-    def combine(s, alpha, beta):
+    def combine(s, scale):
+        two = scale * scale
+        c1 = 2.25 * scale
+        c3 = -2.4375 * scale * two
+        c5 = 1.6875 * scale * (two * two)
+        c7 = -0.5625 * scale * (two * two) * two
+        c9 = 0.0625 * scale * (two * two) * (two * two)
         for r, c in ((0, 0), (0, T), (T, T)):
-            f = alpha * sm[s, r : r + T, c : c + T] - beta * fm[s, r : r + T, c : c + T]
-            fm[s, r : r + T, c : c + T] = f
+            at = (s, slice(r, r + T), slice(c, c + T))
+            f = c1 * sm[at] + c3 * fm[at] + c5 * pw[(0, *at)] + c7 * pw[(1, *at)] + c9 * pw[(2, *at)]
+            fm[at] = f
             put(xs[s], r, c, f)
             if r != c:
                 put(xs[s], c, r, f.T)
 
+    def power(a, b, s, dst, halves=None):
+        def store(m, c, p):
+            dst[s, :m, c : c + T] = p
+            if halves is not None:
+                put(halves, 0, c, p)
+                if c:
+                    put(halves, T, 0, p[:T].T)
+
+        product(a, b, store)
+
     def cube(s):
-        def store(m, c, p):
-            fm[s, :m, c : c + T] = p
-
-        product(xs[s], qs[s], store)
+        power(xs[s], qs[s], s, fm, thirds[s])
+
+    def fourth(s):
+        square(qs[s], fourths[s], ls[s])
+
+    def fifth(s):
+        power(thirds[s], qs[s], s, pw.at[0], fifths[s])
+
+    def seventh(s):
+        power(thirds[s], fourths[s], s, pw.at[1])
+
+    def ninth(s):
+        power(fifths[s], fourths[s], s, pw.at[2])
 
     def advance(s):
         def store(m, c, p):
@@ -239,30 +283,39 @@
         n0 = norm(0)
         if t == 1:
             relay(1, 1)
+        cube(0)
+        fourth(0)
         arrived(t, 1, (0, 1, 2, 4))
         assemble(t, 1)
         n1 = norm(1)
         own1[t] = jnp.broadcast_to(jnp.maximum(n0, n1), (8, 128))
-        for k in range(1, ROWS):
+        for k in row_order:
             maxcp(t, k).start()
-        cube(0)
-        for k in range(1, ROWS):
+        cube(1)
+        fifth(0)
+        fourth(1)
+        seventh(0)
+        for k in row_order:
             maxcp(t, k).wait_recv()
         top = own1[t]
-        for k in range(1, ROWS):
+        for k in row_order:
             top = jnp.maximum(top, mx1[t, k])
         own2[t] = top
-        for k in range(ROWS, ROWS + COLS - 1):
+        for k in col_order:
             maxcp(t, k).start()
-        cube(1)
-        for k in range(ROWS, ROWS + COLS - 1):
+        fifth(1)
+        ninth(0)
+        seventh(1)
+        ninth(1)
+        sent(t)
+        for k in row_order:
+            maxcp(t, k).wait_send()
+        for k in col_order:
             maxcp(t, k).wait_recv()
-            top = jnp.maximum(top, mx2[t, k - ROWS + 1])
-        scale = 1.5 / jnp.sqrt(jnp.sqrt(top + EPS))
-        alpha = (1.5 * scale)[:1, :1]
-        beta = (0.5 * scale * scale * scale)[:1, :1]
-        combine(0, alpha, beta)
-        combine(1, alpha, beta)
+            top = jnp.maximum(top, mx2[t, k - ROWS])
+        scale = (1.5 / jnp.sqrt(jnp.sqrt(top + EPS)))[:1, :1]
+        combine(0, scale)
+        combine(1, scale)
         sq(0)
 
         def body(i, carry):
@@ -272,7 +325,7 @@
             advance(1)
             return carry
 
-        lax.fori_loop(0, 3, body, 0)
+        lax.fori_loop(0, 2, body, 0)
         tail(t, 0)
         send(t + 1, 0)
         sq(1)
@@ -291,14 +344,10 @@
     for s in range(SLOTS):
         finish(s)
 
-    for e in range(STEPS + 1):
-        for s in range(SLOTS):
-            for d in range(5):
-                for q in range(2):
-                    cp(e, d, s, q).wait_send()
     for t in range(STEPS):
-        for k in range(1, ROWS + COLS - 1):
+        for k in col_order:
             maxcp(t, k).wait_send()
+    sent(STEPS)
 
 
 def per_device(hamiltonian, block_lists):
@@ -316,8 +365,9 @@
             pltpu.VMEM((5, SLOTS, 2, B // 2, B), f32),
             pltpu.VMEM((SLOTS, N, N), f32),
             pltpu.VMEM((SLOTS, N, N), f32),
-            halves, halves, mat,
-            halves, halves, mat,
+            pltpu.VMEM((3, SLOTS, N, N), f32),
+            halves, halves, mat, halves, halves, halves,
+            halves, halves, mat, halves, halves, halves,
             pltpu.VMEM((STEPS, SLOTS, 4, B, B), f32),
             pltpu.VMEM((STEPS, SLOTS, B, B), f32),
             pltpu.VMEM((STEPS, 8, 128), f32),
@@ -327,11 +377,11 @@
             pltpu.SemaphoreType.DMA,
             pltpu.SemaphoreType.DMA((3, 5, SLOTS, 2)),
             pltpu.SemaphoreType.DMA((3, 5, SLOTS, 2)),
-            pltpu.SemaphoreType.DMA((STEPS, ROWS + COLS - 1)),
-            pltpu.SemaphoreType.DMA((STEPS, ROWS + COLS - 1)),
+            pltpu.SemaphoreType.DMA((STEPS, ROWS + COLS)),
+            pltpu.SemaphoreType.DMA((STEPS, ROWS + COLS)),
         ],
         compiler_params=pltpu.CompilerParams(collective_id=0, has_side_effects=True),
-    )(block_lists, hamiltonian)
+    )(block_lists.T, hamiltonian)
 
 
 def solution(mesh):

time: 91.4 us -> 84.3 us (0.922)
  Pallas kernels: 86.9 us -> 81.2 us
  local copies, waits for them, and re-layouts: 3.35 us -> 1.87 us
    pallas_call x1, Pallas kernels: 86.9 us -> 81.2 us  [per_device(): pl.pallas_call(kernel, out_shape=jax.ShapeDtypeStruct((SLOTS, 4, B, B), f...]
    unnamed x2 -> x1, local copies, waits for them, and re-layouts: 3.35 us -> 1.87 us
where the time goes in v2:
time: 84.3 us; the launch traced here: 83.1 us
  Pallas kernels  81.2 us (96%)
  local copies, waits for them, and re-layouts  1.87 us (2%)
    pallas_call x1, Pallas kernels, per_device(): pl.pallas_call(kernel, out_shape=jax.ShapeDtypeStruct((SLOTS, 4, B, B), f...  81.2 us
    unnamed x1, local copies, waits for them, and re-layouts  1.87 us

profile of v2, /device:TPU:1, one launch (start us, length us, event | category | flops | bytes accessed | tf_op | source)
XLA Modules:
  0.0 83.1 jit_solution(4629481795732689144)
XLA Ops:
  0.0 81.2 %shard_map.28 = f32[2,4,128,128]{3,2,1,0:T(8,128)} custom-call(s32[4,256]{1,0:T(4,128)} %bitcast.1, f32[2,4,128,128]{3,2,1,0:T(8,128)} %h_any.1), custom_call_target="tpu_custom_call" | custom-call | tf_op jit(solution)/shard_map/pallas_call | solution.py:356
  81.2 1.9 %copy.4 = f32[2,4,128,128]{3,2,1,0:T(8,128)} copy(f32[2,4,128,128]{3,2,1,0:T(8,128)} %shard_map.28) | data formatting | bytes 1048576

commit v3 on v2

--- a/solution.py
+++ b/solution.py
@@ -97,7 +97,10 @@
     for k in row_order:
         pl.semaphore_signal(barrier, inc=1, device_id=row_peer(k), device_id_type=MESH)
 
-    def cp(e, d, s, q):
+    def pieces(e, d):
+        return 4 if d >= 3 and e < STEPS else 2
+
+    def cp(e, d, s, c):
         target = (
             (row, (col + 1) % COLS),
             (row, (col + COLS - 1) % COLS),
@@ -106,6 +109,10 @@
             (row_f, col),
         )[d]
         face = (2, 1, 3, 3, 3)[d]
+        half = B // 2
+        fine = pieces(e, d) == 4
+        q = c // 2 if fine else c
+        part = pl.ds(half * (c % 2), half)
         if d == 4:
             src = rb[e].at[3, s, q]
         elif e == 0:
@@ -113,36 +120,38 @@
         elif e == 1:
             src = dct.at[0, s, face] if q else dg.at[0, s]
         else:
-            src = dct.at[1, s, face, pl.ds(64 * q, 64)]
+            src = dct.at[1, s, face, pl.ds(half * q, half)]
+        dst = rb[e].at[d, s, q]
         return pltpu.make_async_remote_copy(
-            src_ref=src,
-            dst_ref=rb[e].at[d, s, q],
-            send_sem=es.at[e, d, s, q],
-            recv_sem=er.at[e, d, s, q],
+            src_ref=src.at[part] if fine else src,
+            dst_ref=dst.at[part] if fine else dst,
+            send_sem=es.at[e, d, s, c],
+            recv_sem=er.at[e, d, s, c],
             device_id=target,
             device_id_type=MESH,
         )
 
     def send(e, s):
-        for q in range(2):
+        for c in range(4):
             for d in (3, 0, 1, 2):
-                cp(e, d, s, q).start()
+                if c < pieces(e, d):
+                    cp(e, d, s, c).start()
 
     def relay(e, s):
-        for q in range(2):
-            cp(e, 3, s, q).wait_recv()
-            cp(e, 4, s, q).start()
+        for c in range(pieces(e, 3)):
+            cp(e, 3, s, c).wait_recv()
+            cp(e, 4, s, c).start()
 
     def arrived(e, s, dirs):
         for d in dirs:
-            for q in range(2):
-                cp(e, d, s, q).wait_recv()
+            for c in range(pieces(e, d)):
+                cp(e, d, s, c).wait_recv()
 
     def sent(e):
         for s in range(SLOTS):
             for d in range(5):
-                for q in range(2):
-                    cp(e, d, s, q).wait_send()
+                for c in range(pieces(e, d)):
+                    cp(e, d, s, c).wait_send()
 
     def maxcp(t, k):
         if k < ROWS:
@@ -173,9 +182,9 @@
         if t == 0:
             h = hv[s, 0]
             d = 0.5 * (h + h.T)
+            sm[s, blk[0], blk[0]] = d
         else:
-            d = sm[s, blk[0], blk[0]] + dg[0, s]
-        sm[s, blk[0], blk[0]] = d
+            d = sm[s, blk[0], blk[0]]
         put(x, 0, 0, d)
         for k in range(1, 4):
             p = present[s][k]
@@ -184,7 +193,7 @@
                 low = (0.5 * p) * (hv[s, k] + face.T)
                 d = (0.5 * p) * (diag + diag.T)
             else:
-                low = sm[s, blk[k], blk[0]] + (0.5 * p) * (dct[0, s, k].T + face)
+                low = sm[s, blk[k], blk[0]] + (0.5 * p) * face
                 d = sm[s, blk[k], blk[k]] + p * diag
             up = low.T
             sm[s, blk[k], blk[0]] = low
@@ -193,9 +202,21 @@
             put(x, B * k, 0, low)
             put(x, 0, B * k, up)
             put(x, B * k, B * k, d)
-            for i in range(1, 4):
-                if t != 0 and i != k:
-                    put(x, B * k, B * i, jnp.zeros((B, B), f32))
+
+    def prepare(t, s):
+        if t == 0:
+            sm[s, blk[0], blk[0]] = sm[s, blk[0], blk[0]] + dg[0, s]
+        else:
+            out[s, 0] = dg[1, s]
+        for k in range(1, 4):
+            own = (0.5 * present[s][k]) * dct[t, s, k].T
+            if t == 0:
+                sm[s, blk[k], blk[0]] = sm[s, blk[k], blk[0]] + own
+                for i in range(1, 4):
+                    if i != k:
+                        put(xs[s], B * k, B * i, jnp.zeros((B, B), f32))
+            else:
+                out[s, k] = own
 
     def combine(s, scale):
         two = scale * scale
@@ -331,22 +352,22 @@
         sq(1)
         tail(t, 1)
         send(t + 1, 1)
+        prepare(t, 0)
         relay(t + 1, 0)
+        prepare(t, 1)
+        for k in col_order:
+            maxcp(t, k).wait_send()
 
     def finish(s):
         arrived(2, s, (0, 1, 2, 4))
-        out[s, 0] = dg[1, s]
         for k in range(1, 4):
             face = jnp.concatenate([got(2, s, k, 0), got(2, s, k, 1)], 0)
-            out[s, k] = (0.5 * present[s][k]) * (dct[1, s, k].T + face)
+            out[s, k] = out[s, k] + (0.5 * present[s][k]) * face
 
     relay(2, 1)
     for s in range(SLOTS):
         finish(s)
 
-    for t in range(STEPS):
-        for k in col_order:
-            maxcp(t, k).wait_send()
     sent(STEPS)
 
 
@@ -355,7 +376,7 @@
     halves = pltpu.VMEM((N, 2 * N), bf16)
     return pl.pallas_call(
         kernel,
-        out_shape=jax.ShapeDtypeStruct((SLOTS, 4, B, B), f32),
+        out_shape=pltpu.VMEM((SLOTS, 4, B, B), f32),
         in_specs=[pl.BlockSpec(memory_space=pltpu.SMEM), pl.BlockSpec(memory_space=pl.ANY)],
         out_specs=pl.BlockSpec(memory_space=pltpu.VMEM),
         scratch_shapes=[
@@ -375,8 +396,8 @@
             pltpu.VMEM((STEPS, ROWS, 8, 128), f32),
             pltpu.VMEM((STEPS, COLS, 8, 128), f32),
             pltpu.SemaphoreType.DMA,
-            pltpu.SemaphoreType.DMA((3, 5, SLOTS, 2)),
-            pltpu.SemaphoreType.DMA((3, 5, SLOTS, 2)),
+            pltpu.SemaphoreType.DMA((3, 5, SLOTS, 4)),
+            pltpu.SemaphoreType.DMA((3, 5, SLOTS, 4)),
             pltpu.SemaphoreType.DMA((STEPS, ROWS + COLS)),
             pltpu.SemaphoreType.DMA((STEPS, ROWS + COLS)),
         ],

time: 84.3 us -> 82.1 us (0.974)
  Pallas kernels: 81.2 us -> 80.1 us
  local copies, waits for them, and re-layouts: 1.87 us -> 0.8 us
    pallas_call x1, Pallas kernels: 81.2 us -> 80.1 us  [per_device(): pl.pallas_call(kernel, out_shape=pltpu.VMEM((SLOTS, 4, B, B), f32), in_sp...]
    unnamed x1, local copies, waits for them, and re-layouts: 1.87 us -> 0.8 us
where the time goes in v3:
time: 82.1 us; the launch traced here: 80.9 us
  Pallas kernels  80.1 us (98%)
    pallas_call x1, Pallas kernels, per_device(): pl.pallas_call(kernel, out_shape=pltpu.VMEM((SLOTS, 4, B, B), f32), in_sp...  80.1 us

profile of v3, /device:TPU:1, one launch (start us, length us, event | category | flops | bytes accessed | tf_op | source)
XLA Modules:
  0.0 80.9 jit_solution(8076561285593086295)
XLA Ops:
  0.0 80.1 %shard_map.28 = f32[2,4,128,128]{3,2,1,0:T(8,128)S(1)} custom-call(s32[4,256]{1,0:T(4,128)} %bitcast.1, f32[2,4,128,128]{3,2,1,0:T(8,128)} %h_any.1), custom_call_target="tpu_custom_call" | custom-call | tf_op jit(solution)/shard_map/pallas_call | solution.py:377
  80.1 0.8 copy.4

commit v4 on v3

--- a/solution.py
+++ b/solution.py
@@ -302,10 +302,7 @@
         arrived(t, 0, (0, 1, 2, 4))
         assemble(t, 0)
         n0 = norm(0)
-        if t == 1:
-            relay(1, 1)
         cube(0)
-        fourth(0)
         arrived(t, 1, (0, 1, 2, 4))
         assemble(t, 1)
         n1 = norm(1)
@@ -313,6 +310,7 @@
         for k in row_order:
             maxcp(t, k).start()
         cube(1)
+        fourth(0)
         fifth(0)
         fourth(1)
         seventh(0)
@@ -352,9 +350,10 @@
         sq(1)
         tail(t, 1)
         send(t + 1, 1)
+        relay(t + 1, 0)
         prepare(t, 0)
-        relay(t + 1, 0)
         prepare(t, 1)
+        relay(t + 1, 1)
         for k in col_order:
             maxcp(t, k).wait_send()
 
@@ -364,7 +363,6 @@
             face = jnp.concatenate([got(2, s, k, 0), got(2, s, k, 1)], 0)
             out[s, k] = out[s, k] + (0.5 * present[s][k]) * face
 
-    relay(2, 1)
     for s in range(SLOTS):
         finish(s)
 

time: 82.1 us -> 79.4 us (0.967)
  Pallas kernels: 80.1 us -> 77.4 us
    pallas_call x1, Pallas kernels: 80.1 us -> 77.4 us  [per_device(): pl.pallas_call(kernel, out_shape=pltpu.VMEM((SLOTS, 4, B, B), f32), in_sp...]
where the time goes in v4:
time: 79.4 us; the launch traced here: 78.2 us
  Pallas kernels  77.4 us (97%)
  local copies, waits for them, and re-layouts  0.8 us (1%)
    pallas_call x1, Pallas kernels, per_device(): pl.pallas_call(kernel, out_shape=pltpu.VMEM((SLOTS, 4, B, B), f32), in_sp...  77.4 us

profile of v4, /device:TPU:1, one launch (start us, length us, event | category | flops | bytes accessed | tf_op | source)
XLA Modules:
  0.0 78.2 jit_solution(17932998772790860726)
XLA Ops:
  0.0 77.4 %shard_map.28 = f32[2,4,128,128]{3,2,1,0:T(8,128)S(1)} custom-call(s32[4,256]{1,0:T(4,128)} %bitcast.1, f32[2,4,128,128]{3,2,1,0:T(8,128)} %h_any.1), custom_call_target="tpu_custom_call" | custom-call | tf_op jit(solution)/shard_map/pallas_call | solution.py:375
  77.4 0.8 %copy.4 = f32[2,4,128,128]{3,2,1,0:T(8,128)} copy(f32[2,4,128,128]{3,2,1,0:T(8,128)S(1)} %shard_map.28) | data formatting | bytes 1048576

commit v5 on v4

--- a/solution.py
+++ b/solution.py
@@ -98,7 +98,7 @@
         pl.semaphore_signal(barrier, inc=1, device_id=row_peer(k), device_id_type=MESH)
 
     def pieces(e, d):
-        return 4 if d >= 3 and e < STEPS else 2
+        return 4 if d >= 3 else 2
 
     def cp(e, d, s, c):
         target = (
@@ -112,7 +112,8 @@
         half = B // 2
         fine = pieces(e, d) == 4
         q = c // 2 if fine else c
-        part = pl.ds(half * (c % 2), half)
+        size = half if e < STEPS else half // 2
+        part = pl.ds(size * (c % 2), size)
         if d == 4:
             src = rb[e].at[3, s, q]
         elif e == 0:
@@ -306,7 +307,7 @@
         arrived(t, 1, (0, 1, 2, 4))
         assemble(t, 1)
         n1 = norm(1)
-        own1[t] = jnp.broadcast_to(jnp.maximum(n0, n1), (8, 128))
+        own1[t] = jnp.broadcast_to(jnp.maximum(n0, n1), (1, 128))
         for k in row_order:
             maxcp(t, k).start()
         cube(1)
@@ -389,10 +390,10 @@
             halves, halves, mat, halves, halves, halves,
             pltpu.VMEM((STEPS, SLOTS, 4, B, B), f32),
             pltpu.VMEM((STEPS, SLOTS, B, B), f32),
-            pltpu.VMEM((STEPS, 8, 128), f32),
-            pltpu.VMEM((STEPS, 8, 128), f32),
-            pltpu.VMEM((STEPS, ROWS, 8, 128), f32),
-            pltpu.VMEM((STEPS, COLS, 8, 128), f32),
+            pltpu.VMEM((STEPS, 1, 128), f32),
+            pltpu.VMEM((STEPS, 1, 128), f32),
+            pltpu.VMEM((STEPS, ROWS, 1, 128), f32),
+            pltpu.VMEM((STEPS, COLS, 1, 128), f32),
             pltpu.SemaphoreType.DMA,
             pltpu.SemaphoreType.DMA((3, 5, SLOTS, 4)),
             pltpu.SemaphoreType.DMA((3, 5, SLOTS, 4)),

time: 79.4 us -> 79.2 us (level)
  no operation moved by 1% of the time
where the time goes in v5:
time: 79.2 us; the launch traced here: 78 us
  Pallas kernels  77.2 us (97%)
  local copies, waits for them, and re-layouts  0.8 us (1%)
    pallas_call x1, Pallas kernels, per_device(): pl.pallas_call(kernel, out_shape=pltpu.VMEM((SLOTS, 4, B, B), f32), in_sp...  77.2 us

profile of v5, /device:TPU:1, one launch (start us, length us, event | category | flops | bytes accessed | tf_op | source)
XLA Modules:
  0.0 78.0 jit_solution(508347596151942234)
XLA Ops:
  0.0 77.2 %shard_map.28 = f32[2,4,128,128]{3,2,1,0:T(8,128)S(1)} custom-call(s32[4,256]{1,0:T(4,128)} %bitcast.1, f32[2,4,128,128]{3,2,1,0:T(8,128)} %h_any.1), custom_call_target="tpu_custom_call" | custom-call | tf_op jit(solution)/shard_map/pallas_call | solution.py:376
  77.2 0.8 %copy.4 = f32[2,4,128,128]{3,2,1,0:T(8,128)} copy(f32[2,4,128,128]{3,2,1,0:T(8,128)S(1)} %shard_map.28) | data formatting | bytes 1048576
